TPU v7x, 256 devices: a whole 4x4x8 slice. The times are simulated.
256 devices in a mesh: seq: 64 (over x, z, core), tp: 4 (over y).
Axes of the slice: x: 4, y: 4, z: 8, core: 2. Of those that a mesh axis runs over, the one named last changes fastest.
Arguments:
- queries: bfloat16 [65536, 2048], P('seq', 'tp'), may hold values from -6.5 to 6.5
- db_keys: bfloat16 [1024, 128, 2048], P('seq', None, 'tp'), may hold values from -6 to 6
- db_values: bfloat16 [1024, 128, 2048], P('seq', None, 'tp'), may hold values from -12 to 12
- nb_shard: int32 [1024, 2], P('seq'), may hold values from 0 to 63, all different within a row; in each aligned block of 16 rows (0 to 15, 16 to 31, ...) at most 2 rows name the same one
- nb_row: int32 [1024, 2], P('seq'), may hold values from 0 to 15
- out_weight: bfloat16 [2048, 4096], P('seq', 'tp'), may hold values from -0.125 to 0.125
Outputs:
- mixed: bfloat16 [65536, 4096], P('seq', 'tp')
Inputs may be any that keep to these rules, and one draw needn't show every extreme that they name: `nb_shard`: among the 16 blocks of one index of seq no shard is named more than 2 times, a bound that some block reaches in some such group; the 2 shards of one block differ.
All inputs are finite; a program needn't handle non-finite values.
Results may differ from a plain program's by a relative error of at most 0.024.
Values may be sent and summed in bfloat16 or wider, within the bound.
No kernel may reach another device: no remote copies, remote signals or barrier semaphores. Data moves between devices by JAX's collectives and lax.ppermute only.
A program may use at most 192 MiB of HBM per device.

v0:
```python
import jax
import jax.numpy as jnp
from jax import lax
from jax.sharding import PartitionSpec as P

HD = 128
BLOCK = 64
NBR = 2
NLEN = 128


def from_behind(shard, axis, by):
    count = lax.axis_size(axis)
    pairs = [(i, i + by) for i in range(count) if 0 <= i + by < count]
    return lax.ppermute(shard, axis, pairs)


def per_device(queries, db_keys, db_values, nb_shard, nb_row, out_weight):
    score_scale = float(HD) ** (-0.5)
    tok_rows = queries.shape[0]
    feature_cols = queries.shape[1]
    heads_here = feature_cols // HD
    blocks = tok_rows // BLOCK
    shards = lax.axis_size("seq")
    capacity = max(2, 4 * blocks // shards)
    upcoming = from_behind(queries[:BLOCK], "seq", -1)
    extended = jnp.concatenate([queries[BLOCK - 1 :], upcoming[: BLOCK - 1]], axis=0).reshape(
        blocks, BLOCK, feature_cols
    )
    owners = nb_shard.reshape(-1)
    entries = nb_row.reshape(-1)
    requests = owners.shape[0]
    positions = jnp.arange(requests, dtype=jnp.int32)
    same_owner = (owners[:, None] == owners[None, :]) & (positions[None, :] < positions[:, None])
    slot_rank = jnp.sum(same_owner.astype(jnp.int32), axis=1)
    slot_index = owners * capacity + slot_rank
    outgoing = (
        jnp.zeros((shards * capacity, BLOCK, feature_cols), jnp.bfloat16)
        .at[slot_index]
        .set(extended[positions // NBR])
    )
    outgoing = outgoing.reshape(shards, capacity, BLOCK, feature_cols)
    wanted = (
        jnp.zeros((shards * capacity,), jnp.int32)
        .at[slot_index]
        .set(entries)
        .reshape(shards, capacity)
    )
    asked_queries = lax.all_to_all(outgoing, "seq", split_axis=0, concat_axis=0, tiled=True)
    asked_rows = lax.all_to_all(wanted, "seq", split_axis=0, concat_axis=0, tiled=True)
    sources = asked_rows.shape[0]
    slots_in = asked_rows.shape[1]
    key_rows = db_keys[asked_rows].reshape(sources, slots_in, NLEN, heads_here, HD)
    value_rows = db_values[asked_rows].reshape(sources, slots_in, NLEN, heads_here, HD)
    query_heads = asked_queries.reshape(sources, slots_in, BLOCK, heads_here, HD)
    scores = (
        jnp.einsum("scqhd,sckhd->schqk", query_heads, key_rows, preferred_element_type=jnp.float32)
        * score_scale
    )
    row_max = jnp.max(scores, axis=-1, keepdims=True)
    log_total = row_max[..., 0] + jnp.log(jnp.sum(jnp.exp(scores - row_max), axis=-1))
    weights = jnp.exp(scores - log_total[..., None]).astype(jnp.bfloat16)
    partial_value = jnp.einsum(
        "schqk,sckhd->scqhd", weights, value_rows, preferred_element_type=jnp.float32
    )
    partial_value = partial_value.astype(jnp.bfloat16).reshape(
        sources, slots_in, BLOCK, feature_cols
    )
    partials = lax.all_to_all(partial_value, "seq", split_axis=0, concat_axis=0, tiled=True)
    log_totals = lax.all_to_all(
        log_total.astype(jnp.bfloat16), "seq", split_axis=0, concat_axis=0, tiled=True
    ).astype(log_total.dtype)
    partials = partials.reshape(shards * capacity, BLOCK, feature_cols)[slot_index]
    partials = partials.reshape(blocks, NBR, BLOCK, heads_here, HD)
    log_totals = log_totals.reshape(shards * capacity, heads_here, BLOCK)[slot_index]
    log_totals = log_totals.reshape(blocks, NBR, heads_here, BLOCK)
    best_log = jnp.max(log_totals, axis=1, keepdims=True)
    merged_log = best_log + jnp.log(jnp.sum(jnp.exp(log_totals - best_log), axis=1, keepdims=True))
    share = jnp.transpose(jnp.exp(log_totals - merged_log), (0, 1, 3, 2))[..., None]
    attended = jnp.sum(share * partials.astype(jnp.float32), axis=1).astype(jnp.bfloat16)
    attended = attended.reshape(blocks * BLOCK, feature_cols)
    tail_rows = from_behind(attended[-BLOCK:], "seq", 1)
    placed = jnp.concatenate([tail_rows[1:], attended[: tok_rows - (BLOCK - 1)]], axis=0)
    rows_all = lax.all_gather(out_weight, "seq", axis=0, tiled=True)
    own_rows = lax.all_to_all(rows_all, "tp", split_axis=0, concat_axis=1, tiled=True)
    terms = jnp.dot(placed, own_rows, preferred_element_type=jnp.float32)
    mixed = lax.psum_scatter(terms.astype(jnp.bfloat16), "tp", scatter_dimension=1, tiled=True)
    return mixed


def solution(mesh):
    placed = (
        P("seq", "tp"),
        P("seq", None, "tp"),
        P("seq", None, "tp"),
        P("seq", None),
        P("seq", None),
        P("seq", "tp"),
    )
    return jax.shard_map(
        per_device, mesh=mesh, in_specs=placed, out_specs=P("seq", "tp"), check_vma=False
    )
```

profile of v0, /device:TPU:1, one launch (start us, length us, event | category | flops | bytes accessed | tf_op | source)
XLA Modules:
  0.0 664.9 jit_solution(10887075580433408227)
XLA Ops:
  6.5 0.8 broadcast_multiply_fusion
  10.9 13.0 %all-to-all-start.1 = ((s32[64,1,2]{2,1,0:T(1,128)}), s32[64,1,2]{2,1,0:T(1,128)S(1)}, u32[]{:S(2)}, u32[]{:S(2)}) async-start(s32[64,1,2]{2,1,0:T(1,128)} %bitcast.5), calls=%async_computation.1 | async-start | bytes 65536 | tf_op jit(solution)/shard_map/all_to_all | solution.py:50
  23.8 0.8 slice.22
  24.7 2.4 collective-permute-start
  27.0 1.4 slice.21
  28.5 2.0 collective-permute-done
  30.6 2.0 gather_fusion
  32.6 4.2 broadcast_in_dim.4
  36.9 6.3 scatter_fusion
  43.1 9.9 %all-to-all-start = ((bf16[64,2,64,512]{3,2,1,0:T(8,128)(2,1)}), bf16[64,2,64,512]{3,2,1,0:T(8,128)(2,1)}, u32[]{:S(2)}, u32[]{:S(2)}) async-start(bf16[64,2,64,512]{3,2,1,0:T(8,128)(2,1)} %bitcast.66), calls=%async_computation | async-start | bytes 16777216 | tf_op jit(solution)/shard_map/all_to_all | solution.py:49
  53.4 7.8 %gather_fusion.1 = bf16[128,128,512]{2,1,0:T(8,128)(2,1)} fusion(bf16[16,128,512]{2,1,0:T(8,128)(2,1)S(1)} %copy-done, s32[1024]{0:T(1024)S(1)} %pad_clamp_fusion.1), kind=kCustom, calls=%fused_computation.1 | custom fusion | bytes 33554944 | tf_op jit(solution)/shard_map/gather | solution.py:53
  61.2 23.9 %reshape.170 = bf16[64,2,128,4,128]{4,3,2,1,0:T(4,128)(2,1)} reshape(bf16[128,128,512]{2,1,0:T(8,128)(2,1)} %gather_fusion.1) | data formatting | bytes 33554432 | tf_op jit(solution)/shard_map/reshape | solution.py:53
  85.1 7.9 %gather_fusion.3 = bf16[128,128,512]{2,1,0:T(8,128)(2,1)} fusion(bf16[16,128,512]{2,1,0:T(8,128)(2,1)S(1)} %copy-done.2, s32[1024]{0:T(1024)S(1)} %pad_clamp_fusion.1), kind=kCustom, calls=%fused_computation.3 | custom fusion | bytes 33554944 | tf_op jit(solution)/shard_map/gather | solution.py:54
  93.0 23.7 %reshape.174 = bf16[64,2,128,4,128]{4,3,2,1,0:T(4,128)(2,1)} reshape(bf16[128,128,512]{2,1,0:T(8,128)(2,1)} %gather_fusion.3) | data formatting | bytes 33554432 | tf_op jit(solution)/shard_map/reshape | solution.py:54
  116.7 122.1 %all-to-all-done = bf16[64,2,64,512]{3,2,1,0:T(8,128)(2,1)} async-done(((bf16[64,2,64,512]{3,2,1,0:T(8,128)(2,1)}), bf16[64,2,64,512]{3,2,1,0:T(8,128)(2,1)}, u32[]{:S(2)}, u32[]{:S(2)}) %all-to-all-start) | async-done | bytes 8388640 | tf_op jit(solution)/shard_map/all_to_all | solution.py:49
  238.8 19.9 %multiply_reduce_fusion = (f32[64,2,4,64]{3,2,1,0:T(4,128)S(1)}, f32[64,2,4,64,128]{4,3,2,1,0:T(8,128)}) fusion(bf16[64,2,128,4,128]{4,3,2,1,0:T(4,128)(2,1)} %reshape.170, bf16[64,2,64,512]{3,2,1,0:T(8,128)(2,1)} %all-to-all-done), kind=kOutput, calls=%fused_computation.13 | convolution fusion | flops 1082097664 | bytes 42074112 | tf_op jit(solution)/shard_map/scqhd,sckhd->schqk/dot_general | solution.py:57
  258.7 12.6 %exponential_reduce_fusion = f32[64,2,4,64]{3,2,1,0:T(4,128)S(1)} fusion(f32[64,2,4,64,128]{4,3,2,1,0:T(8,128)} %get-tuple-element.8, f32[64,2,4,64]{3,2,1,0:T(4,128)S(1)} %get-tuple-element.7), kind=kLoop, calls=%fused_computation.12 | loop fusion | flops 12550144 | bytes 17039360 | tf_op jit(solution)/shard_map/reduce_sum | solution.py:61
  272.3 5.8 all-to-all-start.2
  278.1 15.7 %convert_bitcast_fusion = bf16[64,2,4,8,8,128]{5,4,3,2,1,0:T(8,128)(2,1)} fusion(bf16[64,2,128,4,128]{4,3,2,1,0:T(4,128)(2,1)} %reshape.174, f32[64,2,4,64,128]{4,3,2,1,0:T(8,128)} %get-tuple-element.8, f32[64,2,4,64]{3,2,1,0:T(4,128)S(1)} %get-tuple-element.6), kind=kOutput, calls=%fused_computation.17 | convolution fusion | flops 1090519040 | bytes 42074112 | tf_op jit(solution)/shard_map/schqk,sckhd->scqhd/dot_general | solution.py:63
  293.8 8.4 %copy.81 = bf16[64,2,4,8,8,128]{5,4,2,3,1,0:T(8,128)(2,1)} copy(bf16[64,2,4,8,8,128]{5,4,3,2,1,0:T(8,128)(2,1)} %convert_bitcast_fusion) | data formatting | bytes 16777216 | tf_op jit(solution)/shard_map/reshape | solution.py:66
  302.2 10.5 %all-to-all-start.3 = ((bf16[64,2,64,512]{3,2,1,0:T(8,128)(2,1)}), bf16[64,2,64,512]{3,2,1,0:T(8,128)(2,1)}, u32[]{:S(2)}, u32[]{:S(2)}) async-start(bf16[64,2,64,512]{3,2,1,0:T(8,128)(2,1)} %bitcast.67), calls=%async_computation.3 | async-start | bytes 16777216 | tf_op jit(solution)/shard_map/all_to_all | solution.py:69
  313.5 104.5 %all-gather.2.cloned.1.call-done = bf16[2048,1024]{1,0:T(8,128)(2,1)} async-done(((bf16[32,1024]{1,0:T(8,128)(2,1)}), bf16[2048,1024]{1,0:T(8,128)(2,1)}) %all-gather.2.cloned.1.call-update) | async-done | bytes 4194320 | tf_op jit(solution)/shard_map/all_gather | solution.py:84
  418.0 92.8 %all-to-all-done.3 = bf16[64,2,64,512]{3,2,1,0:T(8,128)(2,1)} async-done(((bf16[64,2,64,512]{3,2,1,0:T(8,128)(2,1)}), bf16[64,2,64,512]{3,2,1,0:T(8,128)(2,1)}, u32[]{:S(2)}, u32[]{:S(2)}) %all-to-all-start.3) | async-done | bytes 8388640 | tf_op jit(solution)/shard_map/all_to_all | solution.py:69
  510.7 4.9 all-to-all-start.4
  517.1 4.1 gather_fusion.4
  521.2 3.1 reshape.179
  524.2 5.0 multiply_reduce_fusion.1
  529.3 1.9 collective-permute-start.1
  531.2 33.8 %all-to-all-done.4 = bf16[4,512,1024]{2,1,0:T(8,128)(2,1)} async-done(((bf16[4,512,1024]{2,1,0:T(8,128)(2,1)}), bf16[4,512,1024]{2,1,0:T(8,128)(2,1)}, u32[]{:S(2)}, u32[]{:S(2)}) %all-to-all-start.4) | async-done | bytes 4194336 | tf_op jit(solution)/shard_map/all_to_all | solution.py:85
  565.0 6.2 copy.59
  571.6 9.2 %convolution_convert_fusion = bf16[1024,4096]{1,0:T(8,128)(2,1)} fusion(bf16[512,4096]{0,1:T(8,128)(2,1)} %bitcast.71, bf16[961,512]{1,0:T(8,128)(2,1)S(1)} %slice.41, bf16[63,512]{1,0:T(8,128)(2,1)S(1)} %slice.40), kind=kOutput, calls=%fused_computation.20 | convolution fusion | flops 4301258752 | bytes 13631488 | tf_op jit(solution)/shard_map/dot_general | solution.py:86
  580.7 77.3 %reduce-scatter.2.cloned.1.call-done = bf16[1024,1024]{1,0:T(8,128)(2,1)} async-done(((bf16[1024,4096]{1,0:T(8,128)(2,1)}), bf16[1024,1024]{1,0:T(8,128)(2,1)}) %reduce-scatter.2.cloned.1.call-update) | async-done | bytes 2097168 | tf_op jit(solution)/shard_map/reduce_scatter | solution.py:87
  (47 shorter events, 7.2 us)
Async XLA Ops:
  6.5 46.9 %copy-start = (bf16[16,128,512]{2,1,0:T(8,128)(2,1)S(1)}, bf16[16,128,512]{2,1,0:T(8,128)(2,1)}, u32[]{:S(2)}) copy-start(bf16[16,128,512]{2,1,0:T(8,128)(2,1)} %param.7) | copy-start | bytes 6291460
  10.9 32.3 %all-to-all-start.1 = ((s32[64,1,2]{2,1,0:T(1,128)}), s32[64,1,2]{2,1,0:T(1,128)S(1)}, u32[]{:S(2)}, u32[]{:S(2)}) async-start(s32[64,1,2]{2,1,0:T(1,128)} %bitcast.5), calls=%async_computation.1 | async-start | bytes 65536 | tf_op jit(solution)/shard_map/all_to_all | solution.py:50
  24.7 5.9 collective-permute-start
  43.1 195.7 %all-to-all-start = ((bf16[64,2,64,512]{3,2,1,0:T(8,128)(2,1)}), bf16[64,2,64,512]{3,2,1,0:T(8,128)(2,1)}, u32[]{:S(2)}, u32[]{:S(2)}) async-start(bf16[64,2,64,512]{3,2,1,0:T(8,128)(2,1)} %bitcast.66), calls=%async_computation | async-start | bytes 16777216 | tf_op jit(solution)/shard_map/all_to_all | solution.py:49
  61.2 23.9 %copy-start.2 = (bf16[16,128,512]{2,1,0:T(8,128)(2,1)S(1)}, bf16[16,128,512]{2,1,0:T(8,128)(2,1)}, u32[]{:S(2)}) copy-start(bf16[16,128,512]{2,1,0:T(8,128)(2,1)} %param.8) | copy-start | bytes 6291460
  272.3 29.9 %all-to-all-start.2 = ((bf16[64,2,256]{2,1,0:T(2,128)(2,1)}), bf16[64,2,256]{2,1,0:T(2,128)(2,1)S(1)}, u32[]{:S(2)}, u32[]{:S(2)}) async-start(bf16[64,2,256]{2,1,0:T(2,128)(2,1)} %reshape.242), calls=%async_computation.2 | async-start | bytes 131072 | tf_op jit(solution)/shard_map/all_to_all | solution.py:70
  302.2 208.5 %all-to-all-start.3 = ((bf16[64,2,64,512]{3,2,1,0:T(8,128)(2,1)}), bf16[64,2,64,512]{3,2,1,0:T(8,128)(2,1)}, u32[]{:S(2)}, u32[]{:S(2)}) async-start(bf16[64,2,64,512]{3,2,1,0:T(8,128)(2,1)} %bitcast.67), calls=%async_computation.3 | async-start | bytes 16777216 | tf_op jit(solution)/shard_map/all_to_all | solution.py:69
  312.7 105.3 %all-gather.2.cloned.1.call-start = ((), (), s32[]{:S(2)}) async-start(), calls=%async_computation.6 | async-start | bytes 4259840 | tf_op jit(solution)/shard_map/all_gather | solution.py:84
  510.7 54.3 %all-to-all-start.4 = ((bf16[4,512,1024]{2,1,0:T(8,128)(2,1)}), bf16[4,512,1024]{2,1,0:T(8,128)(2,1)}, u32[]{:S(2)}, u32[]{:S(2)}) async-start(bf16[4,512,1024]{2,1,0:T(8,128)(2,1)} %bitcast.70), calls=%async_computation.4 | async-start | bytes 8388608 | tf_op jit(solution)/shard_map/all_to_all | solution.py:85
  515.7 142.4 %reduce-scatter.2.cloned.1.call-start = ((), (), s32[]{:S(2)}) async-start(), calls=%async_computation.7 | async-start | bytes 10485760 | tf_op jit(solution)/shard_map/reduce_scatter | solution.py:87
  529.3 42.2 %collective-permute-start.1 = (bf16[64,512]{1,0:T(8,128)(2,1)S(1)}, bf16[64,512]{1,0:T(8,128)(2,1)S(1)}, u32[]{:S(2)}, u32[]{:S(2)}) collective-permute-start(bf16[64,512]{1,0:T(8,128)(2,1)S(1)} %bitcast.78), channel_id=1, source_target_pairs={{0,4},{4,8},{8,12},{12,16},{16,20},{20,24},{24,28},{28,32},{32,36}... | collective-permute-start | bytes 196616 | tf_op jit(solution)/shard_map/ppermute | solution.py:15
  571.5 86.5 %copy-start.1 = (bf16[16,128,512]{2,1,0:T(8,128)(2,1)S(1)}, bf16[16,128,512]{2,1,0:T(8,128)(2,1)}, u32[]{:S(2)}) copy-start(bf16[16,128,512]{2,1,0:T(8,128)(2,1)} %param.7) | copy-start | bytes 6291460
Sparse Core Ops, SparseCore 0:
  316.3 101.6 all-gather.1
  580.9 77.1 reduce-scatter.1
where the time goes:
time: 667 us; the launch traced here: 665 us
  waiting for transfers between devices  433 us (65%)
  local copies, waits for them, and re-layouts  106 us (16%)
  starting transfers between devices  48.5 us (7%)
  matrix products  44.8 us (7%)
  other arithmetic  19 us (3%)
  between operations  13.7 us (2%)
    all_to_all x1, waiting for transfers between devices, per_device(): lax.all_to_all(outgoing, 'seq', split_axis=0, concat_axis=0, tiled=True)  122 us
    all_gather x1, waiting for transfers between devices, per_device(): rows_all = lax.all_gather(out_weight, 'seq', axis=0, tiled=True)  105 us
    all_to_all x1, waiting for transfers between devices, per_device(): lax.all_to_all(partial_value, 'seq', split_axis=0, concat_axis=0, tiled=T...  92.8 us
    reduce_scatter x1, waiting for transfers between devices, per_device(): lax.psum_scatter(terms.astype(jnp.bfloat16), 'tp', scatter_dimension=1, t...  77.3 us
    all_to_all x1, waiting for transfers between devices, per_device(): lax.all_to_all(rows_all, 'tp', split_axis=0, concat_axis=1, tiled=True)  33.8 us
    reshape x1, local copies, waits for them, and re-layouts, per_device(): db_keys[asked_rows].reshape(sources, slots_in, NLEN, heads_here, HD)  23.9 us
    reshape x1, local copies, waits for them, and re-layouts, per_device(): db_values[asked_rows].reshape(sources, slots_in, NLEN, heads_here, HD)  23.7 us
    dot_general x1, matrix products, per_device(): jnp.einsum('scqhd,sckhd->schqk', query_heads, key_rows, preferred_element...  19.9 us
  transfers between devices with their start and end apart: 9, of which 6 were waited for; matrix products, arithmetic and copies ran while one was open for 18% of the time, Pallas kernels for 0%

commit v1 on v0

v1 whole, which is shorter than its diff:
```python
import jax
import jax.numpy as jnp
from jax import lax
from jax.experimental import pallas as pl
from jax.experimental.pallas import tpu as pltpu
from jax.sharding import PartitionSpec as P

HD = 128
BLOCK = 64
NBR = 2
NLEN = 128
PAIR = 2 * HD
SLOTS_STEP = 8


def from_behind(shard, axis, by):
    count = lax.axis_size(axis)
    pairs = [(i, i + by) for i in range(count) if 0 <= i + by < count]
    return lax.ppermute(shard, axis, pairs)


def attend_body(rows_ref, q_ref, k_ref, v_ref, out_ref, log_ref):
    step = pl.program_id(0)
    first_head = lax.broadcasted_iota(jnp.int32, (NLEN, 2 * BLOCK), 1) < BLOCK
    nt = (((1,), (1,)), ((), ()))
    for j in range(SLOTS_STEP):
        row = rows_ref[step * SLOTS_STEP + j]
        q2 = jnp.concatenate([q_ref[j, :, :HD], q_ref[j, :, HD:]], axis=0)
        s0 = lax.dot_general(k_ref[row, :, :HD], q2, nt, preferred_element_type=jnp.float32)
        s1 = lax.dot_general(k_ref[row, :, HD:], q2, nt, preferred_element_type=jnp.float32)
        s = jnp.where(first_head, s0, s1) * (float(HD) ** -0.5)
        top = jnp.max(s, axis=0, keepdims=True)
        e = jnp.exp(s - top)
        total = jnp.sum(e, axis=0, keepdims=True)
        log_ref[pl.ds(j, 1), :] = top + jnp.log(total)
        w = jnp.transpose(e * (1.0 / total)).astype(jnp.bfloat16)
        out_ref[j, :, :HD] = jnp.dot(
            w[:BLOCK], v_ref[row, :, :HD], preferred_element_type=jnp.float32
        ).astype(jnp.bfloat16)
        out_ref[j, :, HD:] = jnp.dot(
            w[BLOCK:], v_ref[row, :, HD:], preferred_element_type=jnp.float32
        ).astype(jnp.bfloat16)


def attend(rows, q, k, v, chunk):
    slots = q.shape[0]
    entries = k.shape[0]
    return pl.pallas_call(
        attend_body,
        grid_spec=pltpu.PrefetchScalarGridSpec(
            num_scalar_prefetch=1,
            grid=(slots // SLOTS_STEP,),
            in_specs=[
                pl.BlockSpec((SLOTS_STEP, BLOCK, PAIR), lambda i, r: (i, 0, 0)),
                pl.BlockSpec((entries, NLEN, PAIR), lambda i, r: (0, 0, chunk)),
                pl.BlockSpec((entries, NLEN, PAIR), lambda i, r: (0, 0, chunk)),
            ],
            out_specs=[
                pl.BlockSpec((SLOTS_STEP, BLOCK, PAIR), lambda i, r: (i, 0, 0)),
                pl.BlockSpec((SLOTS_STEP, 2 * BLOCK), lambda i, r: (i, 0)),
            ],
        ),
        out_shape=[
            jax.ShapeDtypeStruct((slots, BLOCK, PAIR), jnp.bfloat16),
            jax.ShapeDtypeStruct((slots, 2 * BLOCK), jnp.float32),
        ],
        name="attend",
    )(rows, q, k, v)


def merge_body(slot_ref, first_ref, second_ref, log_ref, out_ref):
    u = pl.program_id(0)
    l0 = log_ref[pl.ds(slot_ref[2 * u], 1), :]
    l1 = log_ref[pl.ds(slot_ref[2 * u + 1], 1), :]
    best = jnp.maximum(l0, l1)
    e0 = jnp.exp(l0 - best)
    e1 = jnp.exp(l1 - best)
    inv = 1.0 / (e0 + e1)
    side = 2 * BLOCK
    c0 = jnp.transpose(jnp.broadcast_to(e0 * inv, (side, side)))
    c1 = jnp.transpose(jnp.broadcast_to(e1 * inv, (side, side)))
    p0 = first_ref[0].astype(jnp.float32)
    p1 = second_ref[0].astype(jnp.float32)
    out_ref[:, :HD] = (c0[:BLOCK] * p0[:, :HD] + c1[:BLOCK] * p1[:, :HD]).astype(jnp.bfloat16)
    out_ref[:, HD:] = (c0[BLOCK:] * p0[:, HD:] + c1[BLOCK:] * p1[:, HD:]).astype(jnp.bfloat16)


def merge(slot_index, partials, logs):
    blocks = slot_index.shape[0] // NBR
    slots = partials.shape[0]
    return pl.pallas_call(
        merge_body,
        grid_spec=pltpu.PrefetchScalarGridSpec(
            num_scalar_prefetch=1,
            grid=(blocks,),
            in_specs=[
                pl.BlockSpec((1, BLOCK, PAIR), lambda u, s: (s[2 * u], 0, 0)),
                pl.BlockSpec((1, BLOCK, PAIR), lambda u, s: (s[2 * u + 1], 0, 0)),
                pl.BlockSpec((slots, 2 * BLOCK), lambda u, s: (0, 0)),
            ],
            out_specs=pl.BlockSpec((BLOCK, PAIR), lambda u, s: (u, 0)),
        ),
        out_shape=jax.ShapeDtypeStruct((blocks * BLOCK, PAIR), jnp.bfloat16),
        name="merge",
    )(slot_index, partials, partials, logs)


def per_device(queries, db_keys, db_values, nb_shard, nb_row, out_weight):
    tok_rows = queries.shape[0]
    feature_cols = queries.shape[1]
    chunks = feature_cols // PAIR
    blocks = tok_rows // BLOCK
    shards = lax.axis_size("seq")
    groups = lax.axis_size("tp")
    capacity = max(2, 4 * blocks // shards)
    slots = shards * capacity
    upcoming = from_behind(queries[:BLOCK], "seq", -1)
    owners = nb_shard.reshape(-1)
    entries = nb_row.reshape(-1)
    requests = owners.shape[0]
    positions = jnp.arange(requests, dtype=jnp.int32)
    same_owner = (owners[:, None] == owners[None, :]) & (positions[None, :] < positions[:, None])
    slot_rank = jnp.sum(same_owner.astype(jnp.int32), axis=1)
    slot_index = owners * capacity + slot_rank
    holds = slot_index[None, :] == jnp.arange(slots, dtype=jnp.int32)[:, None]
    wanted = jnp.sum(jnp.where(holds, entries[None, :], 0), axis=1)
    block_of = jnp.sum(jnp.where(holds, (positions // NBR)[None, :], 0), axis=1)
    rows = lax.all_to_all(
        wanted.reshape(shards, capacity), "seq", split_axis=0, concat_axis=0, tiled=True
    ).reshape(-1)
    extended = jnp.concatenate([queries[BLOCK - 1 :], upcoming[: BLOCK - 1]], axis=0).reshape(
        blocks, BLOCK, feature_cols
    )
    asked = []
    for c in range(chunks):
        outgoing = extended[:, :, c * PAIR : (c + 1) * PAIR][block_of]
        asked.append(
            lax.all_to_all(
                outgoing.reshape(shards, capacity, BLOCK, PAIR),
                "seq",
                split_axis=0,
                concat_axis=0,
                tiled=True,
            )
        )
    rows_all = lax.all_gather(out_weight, "seq", axis=0, tiled=True)
    weight = rows_all.reshape(groups, chunks, PAIR, out_weight.shape[1])
    returned = []
    all_logs = []
    for c in range(chunks):
        part, logs = attend(rows, asked[c].reshape(slots, BLOCK, PAIR), db_keys, db_values, c)
        all_logs.append(logs.astype(jnp.bfloat16))
        returned.append(
            lax.all_to_all(
                part.reshape(shards, capacity, BLOCK, PAIR),
                "seq",
                split_axis=0,
                concat_axis=0,
                tiled=True,
            )
        )
    logs_back = lax.all_to_all(
        jnp.concatenate(all_logs, axis=1).reshape(shards, capacity, chunks * 2 * BLOCK),
        "seq",
        split_axis=0,
        concat_axis=0,
        tiled=True,
    ).reshape(slots, chunks * 2 * BLOCK)
    mixed = None
    for c in range(chunks):
        attended = merge(
            slot_index,
            returned[c].reshape(slots, BLOCK, PAIR),
            logs_back[:, c * 2 * BLOCK : (c + 1) * 2 * BLOCK].astype(jnp.float32),
        )
        tail_rows = from_behind(attended[-BLOCK:], "seq", 1)
        placed = jnp.concatenate([tail_rows[1:], attended[: tok_rows - (BLOCK - 1)]], axis=0)
        placed_all = lax.all_gather(placed, "tp", axis=1, tiled=True)
        term = jnp.dot(
            placed_all,
            weight[:, c].reshape(groups * PAIR, -1),
            preferred_element_type=jnp.float32,
        )
        mixed = term if mixed is None else mixed + term
    return mixed.astype(jnp.bfloat16)


def solution(mesh):
    placed = (
        P("seq", "tp"),
        P("seq", None, "tp"),
        P("seq", None, "tp"),
        P("seq", None),
        P("seq", None),
        P("seq", "tp"),
    )
    return jax.shard_map(
        per_device, mesh=mesh, in_specs=placed, out_specs=P("seq", "tp"), check_vma=False
    )
```

time: 667 us -> 602 us (0.903)
  Pallas kernels: 0 us -> 107 us
  local copies, waits for them, and re-layouts: 106 us -> 19.6 us
  waiting for transfers between devices: 433 us -> 381 us
  matrix products: 44.8 us -> 13 us
  blocking collectives: 0 us -> 15.3 us
  other arithmetic: 19 us -> 5.3 us
    pallas_call x0 -> x4, Pallas kernels: none -> 107 us  [the longest x2 87.6 us: attend(): pl.pallas_call(attend_body, grid_spec=pltpu.PrefetchScalarGridSpec(num_sc...]
    all_gather x1, waiting for transfers between devices: 105 us -> 0.02 us  [per_device(): rows_all = lax.all_gather(out_weight, 'seq', axis=0, tiled=True)]
    reduce_scatter x1 -> x0, waiting for transfers between devices: 77.3 us -> none  [per_device(): lax.psum_scatter(terms.astype(jnp.bfloat16), 'tp', scatter_dimension=1, t...]
    ppermute x2 -> x3, waiting for transfers between devices: 2.04 us -> 73 us  [from_behind(): return lax.ppermute(shard, axis, pairs)]
    reshape x4, local copies, waits for them, and re-layouts: 56 us -> 0.88 us  [the longest x1 0.72 us: per_device(): rows = lax.all_to_all(wanted.reshape(shards, capacity), 'seq', split_axis...]
    all_gather x0 -> x2, waiting for transfers between devices: none -> 46.3 us  [per_device(): placed_all = lax.all_gather(placed, 'tp', axis=1, tiled=True)]
    dot_general x3 -> x2, matrix products: 44.8 us -> 13 us  [per_device(): jnp.dot(placed_all, weight[:, c].reshape(groups * PAIR, -1), preferred_el...]
    reduce_sum x3 -> x1, other arithmetic: 17.7 us -> 0.1 us  [per_device(): block_of = jnp.sum(jnp.where(holds, (positions // NBR)[None, :], 0), axis=1)]
  transfers between devices with their start and end apart: 9 -> 11, of which waited for: 6 -> 8; matrix products, arithmetic and copies ran while one was open for 18% -> 5% of each run, Pallas kernels for 0% -> 11%
where the time goes in v1:
time: 602 us; the launch traced here: 599 us
  waiting for transfers between devices  381 us (63%)
  Pallas kernels  107 us (18%)
  starting transfers between devices  43.9 us (7%)
  local copies, waits for them, and re-layouts  19.6 us (3%)
  blocking collectives  15.3 us (3%)
  between operations  13.3 us (2%)
  matrix products  13 us (2%)
    all_to_all x2, waiting for transfers between devices, per_device(): lax.all_to_all(outgoing.reshape(shards, capacity, BLOCK, PAIR), 'seq', sp...  142 us
    all_to_all x2, waiting for transfers between devices, per_device(): lax.all_to_all(part.reshape(shards, capacity, BLOCK, PAIR), 'seq', split_...  114 us
    pallas_call x2, Pallas kernels, attend(): pl.pallas_call(attend_body, grid_spec=pltpu.PrefetchScalarGridSpec(num_sc...  87.6 us
    ppermute x3, waiting for transfers between devices, from_behind(): return lax.ppermute(shard, axis, pairs)  73 us
    all_gather x2, waiting for transfers between devices, per_device(): placed_all = lax.all_gather(placed, 'tp', axis=1, tiled=True)  46.3 us
    pallas_call x2, Pallas kernels, merge(): pl.pallas_call(merge_body, grid_spec=pltpu.PrefetchScalarGridSpec(num_sca...  19.8 us
    all_to_all x1, blocking collectives, per_device(): lax.all_to_all(jnp.concatenate(all_logs, axis=1).reshape(shards, capacity...  15.3 us
    dot_general x2, matrix products, per_device(): jnp.dot(placed_all, weight[:, c].reshape(groups * PAIR, -1), preferred_el...  13 us
  transfers between devices with their start and end apart: 11, of which 8 were waited for; matrix products, arithmetic and copies ran while one was open for 5% of the time, Pallas kernels for 11%

profile of v1, /device:TPU:1, one launch (start us, length us, event | category | flops | bytes accessed | tf_op | source)
XLA Modules:
  0.0 598.6 jit_solution(14625739898862245747)
XLA Ops:
  7.4 5.1 collective-permute-start
  15.2 9.9 %all-to-all-start = ((s32[64,1,2]{2,1,0:T(1,128)}), s32[64,1,2]{2,1,0:T(1,128)S(1)}, u32[]{:S(2)}, u32[]{:S(2)}) async-start(s32[64,1,2]{2,1,0:T(1,128)} %bitcast), calls=%async_computation | async-start | bytes 65536 | tf_op jit(solution)/shard_map/all_to_all | solution.py:128
  25.1 1.4 slice.45
  26.8 2.8 gather_fusion
  29.6 4.8 all-to-all-done
  34.4 5.8 all-to-all-start.1
  40.1 2.7 gather_fusion.1
  42.9 93.1 %all-to-all-done.1 = bf16[64,2,64,256]{3,2,1,0:T(8,128)(2,1)} async-done(((bf16[64,2,64,256]{3,2,1,0:T(8,128)(2,1)}), bf16[64,2,64,256]{3,2,1,0:T(8,128)(2,1)}, u32[]{:S(2)}, u32[]{:S(2)}) %all-to-all-start.1) | async-done | bytes 4194336 | tf_op jit(solution)/shard_map/all_to_all | solution.py:138
  136.0 6.0 %all-to-all-start.3 = ((bf16[64,2,64,256]{3,2,1,0:T(8,128)(2,1)}), bf16[64,2,64,256]{3,2,1,0:T(8,128)(2,1)}, u32[]{:S(2)}, u32[]{:S(2)}) async-start(bf16[64,2,64,256]{3,2,1,0:T(8,128)(2,1)} %bitcast.22), calls=%async_computation.3 | async-start | bytes 8388608 | tf_op jit(solution)/shard_map/all_to_all | solution.py:138
  144.0 43.8 %attend.2 = (bf16[128,64,256]{2,1,0:T(8,128)(2,1)}, f32[128,128]{1,0:T(8,128)}) custom-call(s32[128]{0:T(128)} %reshape.85.rows_ref, bf16[128,64,256]{2,1,0:T(8,128)(2,1)} %bitcast.5.q_ref, bf16[16,128,512]{2,1,0:T(8,128)(2,1)} %k_ref.3, bf16[16,128,512]{2,1,0:T(8,128)(2,1)} %v_ref.3), custom_call_target="tpu_custom_call" | custom-call | tf_op jit(solution)/shard_map/attend/pallas_call | solution.py:48
  187.8 0.8 convert_element_type.19
  188.6 49.2 %all-to-all-done.3 = bf16[64,2,64,256]{3,2,1,0:T(8,128)(2,1)} async-done(((bf16[64,2,64,256]{3,2,1,0:T(8,128)(2,1)}), bf16[64,2,64,256]{3,2,1,0:T(8,128)(2,1)}, u32[]{:S(2)}, u32[]{:S(2)}) %all-to-all-start.3) | async-done | bytes 4194336 | tf_op jit(solution)/shard_map/all_to_all | solution.py:138
  237.8 43.8 %attend.3 = (bf16[128,64,256]{2,1,0:T(8,128)(2,1)}, f32[128,128]{1,0:T(8,128)}) custom-call(s32[128]{0:T(128)} %reshape.85.rows_ref, bf16[128,64,256]{2,1,0:T(8,128)(2,1)} %bitcast.9.q_ref, bf16[16,128,512]{2,1,0:T(8,128)(2,1)} %k_ref.3, bf16[16,128,512]{2,1,0:T(8,128)(2,1)} %v_ref.3), custom_call_target="tpu_custom_call" | custom-call | tf_op jit(solution)/shard_map/attend/pallas_call | solution.py:48
  282.6 15.3 %all_to_all.34 = bf16[64,2,256]{2,1,0:T(2,128)(2,1)S(1)} all-to-all(bf16[64,2,256]{2,1,0:T(2,128)(2,1)S(1)} %reshape.93), channel_id=1, replica_groups=mesh['seq'=64,'tp'=4] {'seq'}, dimensions={0} | all-to-all | bytes 131072 | tf_op jit(solution)/shard_map/all_to_all | solution.py:162
  297.8 5.4 all-to-all-start.5
  304.0 107.5 %all-to-all-done.5 = bf16[64,2,64,256]{3,2,1,0:T(8,128)(2,1)} async-done(((bf16[64,2,64,256]{3,2,1,0:T(8,128)(2,1)}), bf16[64,2,64,256]{3,2,1,0:T(8,128)(2,1)}, u32[]{:S(2)}, u32[]{:S(2)}) %all-to-all-start.5) | async-done | bytes 4194336 | tf_op jit(solution)/shard_map/all_to_all | solution.py:154
  411.5 6.0 %all-to-all-start.2 = ((bf16[64,2,64,256]{3,2,1,0:T(8,128)(2,1)}), bf16[64,2,64,256]{3,2,1,0:T(8,128)(2,1)}, u32[]{:S(2)}, u32[]{:S(2)}) async-start(bf16[64,2,64,256]{3,2,1,0:T(8,128)(2,1)} %bitcast.25), calls=%async_computation.2 | async-start | bytes 8388608 | tf_op jit(solution)/shard_map/all_to_all | solution.py:154
  418.2 9.9 %merge.3 = bf16[1024,256]{1,0:T(8,128)(2,1)} custom-call(s32[32]{0:T(128)} %copy-done, bf16[128,64,256]{2,1,0:T(8,128)(2,1)} %bitcast.13.first_ref.second_ref, bf16[128,64,256]{2,1,0:T(8,128)(2,1)} %bitcast.13.first_ref.second_ref, f32[128,128]{1,0:T(8,128)} %get-tuple-element.20.log_ref), custom_call_target="tpu_custom_call" | custom-call | tf_op jit(solution)/shard_map/merge/pallas_call | solution.py:91
  428.9 3.5 collective-permute-start.2
  432.4 1.1 slice.75
  433.5 73.0 %collective-permute-done.2 = bf16[64,256]{1,0:T(8,128)(2,1)S(1)} collective-permute-done((bf16[64,256]{1,0:T(8,128)(2,1)S(1)}, bf16[64,256]{1,0:T(8,128)(2,1)S(1)}, u32[]{:S(2)}, u32[]{:S(2)}) %collective-permute-start.2) | collective-permute-done | bytes 32800 | tf_op jit(solution)/shard_map/ppermute | solution.py:19
  506.5 0.9 pad_maximum_fusion.2
  507.5 6.2 %all-to-all-done.2 = bf16[64,2,64,256]{3,2,1,0:T(8,128)(2,1)} async-done(((bf16[64,2,64,256]{3,2,1,0:T(8,128)(2,1)}), bf16[64,2,64,256]{3,2,1,0:T(8,128)(2,1)}, u32[]{:S(2)}, u32[]{:S(2)}) %all-to-all-start.2) | async-done | bytes 4194336 | tf_op jit(solution)/shard_map/all_to_all | solution.py:154
  513.7 9.9 %merge.2 = bf16[1024,256]{1,0:T(8,128)(2,1)} custom-call(s32[32]{0:T(128)} %copy-done, bf16[128,64,256]{2,1,0:T(8,128)(2,1)} %bitcast.7.first_ref.second_ref, bf16[128,64,256]{2,1,0:T(8,128)(2,1)} %bitcast.7.first_ref.second_ref, f32[128,128]{1,0:T(8,128)} %get-tuple-element.19.log_ref), custom_call_target="tpu_custom_call" | custom-call | tf_op jit(solution)/shard_map/merge/pallas_call | solution.py:91
  524.3 2.1 collective-permute-start.1
  526.4 1.1 slice.70
  527.5 0.9 pad_maximum_fusion.1
  528.5 4.2 fusion.2
  532.7 13.5 %all-gather.8.cloned.1.call-done = bf16[1024,1024]{1,0:T(8,128)(2,1)} async-done(((bf16[1024,256]{1,0:T(8,128)(2,1)}), bf16[1024,1024]{1,0:T(8,128)(2,1)}) %all-gather.8.cloned.1.call-update) | async-done | bytes 2097168 | tf_op jit(solution)/shard_map/all_gather | solution.py:178
  546.3 6.5 %fusion.4 = f32[1024,1024]{1,0:T(8,128)} fusion(bf16[1024,1024]{1,0:T(8,128)(2,1)} %all-gather.8.cloned.1.call-done, bf16[1024,1024]{1,0:T(8,128)(2,1)} %bitcast.29), kind=kOutput, calls=%fused_computation.25 | convolution fusion | flops 2147483648 | bytes 8388608 | tf_op jit(solution)/shard_map/dot_general | solution.py:179
  552.8 32.8 %all-gather.4.cloned.1.call-done = bf16[1024,1024]{1,0:T(8,128)(2,1)} async-done(((bf16[1024,256]{1,0:T(8,128)(2,1)}), bf16[1024,1024]{1,0:T(8,128)(2,1)}) %all-gather.4.cloned.1.call-update) | async-done | bytes 2097168 | tf_op jit(solution)/shard_map/all_gather | solution.py:178
  585.6 6.5 %add_convert_fusion = bf16[1024,1024]{1,0:T(8,128)(2,1)} fusion(f32[1024,1024]{1,0:T(8,128)} %fusion.4, bf16[1024,1024]{1,0:T(8,128)(2,1)} %all-gather.4.cloned.1.call-done, bf16[1024,1024]{1,0:T(8,128)(2,1)S(1)} %bitcast.28), kind=kOutput, calls=%fused_computation.2 | convolution fusion | flops 2149580800 | bytes 10485760 | tf_op jit(solution)/shard_map/dot_general | solution.py:179
  (36 shorter events, 9.8 us)
Async XLA Ops:
  7.4 19.2 %collective-permute-start = (bf16[64,512]{1,0:T(8,128)(2,1)S(1)}, bf16[64,512]{1,0:T(8,128)(2,1)S(1)}, u32[]{:S(2)}, u32[]{:S(2)}) collective-permute-start(bf16[64,512]{1,0:T(8,128)(2,1)S(1)} %slice.46), channel_id=1, source_target_pairs={{4,0},{8,4},{12,8},{16,12},{20,16},{24,20},{28,24},{32,28},{36,32}... | collective-permute-start | bytes 196616 | tf_op jit(solution)/shard_map/ppermute | solution.py:19
  13.5 13.2 %copy-start = (s32[32]{0:T(128)}, s32[32]{0:T(128)S(1)}, u32[]{:S(2)}) copy-start(s32[32]{0:T(128)S(1)} %get-tuple-element.22.slot_ref) | copy-start | bytes 388
  15.2 19.1 %all-to-all-start = ((s32[64,1,2]{2,1,0:T(1,128)}), s32[64,1,2]{2,1,0:T(1,128)S(1)}, u32[]{:S(2)}, u32[]{:S(2)}) async-start(s32[64,1,2]{2,1,0:T(1,128)} %bitcast), calls=%async_computation | async-start | bytes 65536 | tf_op jit(solution)/shard_map/all_to_all | solution.py:128
  34.4 101.6 %all-to-all-start.1 = ((bf16[64,2,64,256]{3,2,1,0:T(8,128)(2,1)}), bf16[64,2,64,256]{3,2,1,0:T(8,128)(2,1)}, u32[]{:S(2)}, u32[]{:S(2)}) async-start(bf16[64,2,64,256]{3,2,1,0:T(8,128)(2,1)} %bitcast.23), calls=%async_computation.1 | async-start | bytes 8388608 | tf_op jit(solution)/shard_map/all_to_all | solution.py:138
  136.0 101.9 %all-to-all-start.3 = ((bf16[64,2,64,256]{3,2,1,0:T(8,128)(2,1)}), bf16[64,2,64,256]{3,2,1,0:T(8,128)(2,1)}, u32[]{:S(2)}, u32[]{:S(2)}) async-start(bf16[64,2,64,256]{3,2,1,0:T(8,128)(2,1)} %bitcast.22), calls=%async_computation.3 | async-start | bytes 8388608 | tf_op jit(solution)/shard_map/all_to_all | solution.py:138
  297.8 113.6 %all-to-all-start.5 = ((bf16[64,2,64,256]{3,2,1,0:T(8,128)(2,1)}), bf16[64,2,64,256]{3,2,1,0:T(8,128)(2,1)}, u32[]{:S(2)}, u32[]{:S(2)}) async-start(bf16[64,2,64,256]{3,2,1,0:T(8,128)(2,1)} %bitcast.26), calls=%async_computation.5 | async-start | bytes 8388608 | tf_op jit(solution)/shard_map/all_to_all | solution.py:154
  303.3 225.2 %all-gather.6.cloned.1.call-start = ((), (), s32[]{:S(2)}) async-start(), calls=%async_computation.7 | async-start | bytes 4259840 | tf_op jit(solution)/shard_map/all_gather | solution.py:146
  411.5 102.2 %all-to-all-start.2 = ((bf16[64,2,64,256]{3,2,1,0:T(8,128)(2,1)}), bf16[64,2,64,256]{3,2,1,0:T(8,128)(2,1)}, u32[]{:S(2)}, u32[]{:S(2)}) async-start(bf16[64,2,64,256]{3,2,1,0:T(8,128)(2,1)} %bitcast.25), calls=%async_computation.2 | async-start | bytes 8388608 | tf_op jit(solution)/shard_map/all_to_all | solution.py:154
  417.5 128.8 %all-gather.8.cloned.1.call-start = ((), (), s32[]{:S(2)}) async-start(), calls=%async_computation.8 | async-start | bytes 2621440 | tf_op jit(solution)/shard_map/all_gather | solution.py:178
  428.9 77.6 %collective-permute-start.2 = (bf16[64,256]{1,0:T(8,128)(2,1)S(1)}, bf16[64,256]{1,0:T(8,128)(2,1)S(1)}, u32[]{:S(2)}, u32[]{:S(2)}) collective-permute-start(bf16[64,256]{1,0:T(8,128)(2,1)S(1)} %slice.73), channel_id=1, source_target_pairs={{0,4},{4,8},{8,12},{12,16},{16,20},{20,24},{24,28},{28,32},{32,36}... | collective-permute-start | bytes 98312 | tf_op jit(solution)/shard_map/ppermute | solution.py:19
  507.4 78.1 %all-gather.4.cloned.1.call-start = ((), (), s32[]{:S(2)}) async-start(), calls=%async_computation.6 | async-start | bytes 2621440 | tf_op jit(solution)/shard_map/all_gather | solution.py:178
  524.3 3.2 collective-permute-start.1
Sparse Core Ops, SparseCore 0:
  306.9 98.6 all-gather.5
  507.6 38.6 all-gather.7
  548.1 37.4 all-gather.3
